TPU v7x, 256 devices: a whole 4x4x8 slice. The times are simulated.
256 devices in a mesh: section: 16 (over z_lo, x), ctx: 16 (over z_hi, y, core).
Axes of the slice: x: 4, y: 4, z: 8 (z_hi: 2, z_lo: 4; z = z_hi * 4 + z_lo), core: 2. Of those that a mesh axis runs over, the one named last changes fastest.
Arguments:
- queries: bfloat16 [16, 4096, 16, 128], P('section', 'ctx'), may hold values from -12 to 12
- keys: bfloat16 [16, 4096, 128], P('section', 'ctx'), may hold values from -6 to 6
- values: bfloat16 [16, 4096, 128], P('section', 'ctx'), may hold values from -6 to 6
- outputs: bfloat16 [16, 4096, 16, 128], P('section', 'ctx'), may hold values from -6 to 6, as said below
- grad_held: bfloat16 [16, 4096, 16, 128], P('section', 'ctx'), may hold values from -24 to 24
- lse: float32 [16, 16, 4096], P('section', None, 'ctx'), as said below
- span_start: int32 [32], replicated, may hold values from 0 to 3968, as said below
Outputs:
- query_grad: bfloat16 [16, 4096, 16, 128], P('section', 'ctx')
- key_grad: bfloat16 [16, 4096, 128], P('section', 'ctx')
- value_grad: bfloat16 [16, 4096, 128], P('section', 'ctx')
Inputs may be any that keep to these rules, and one draw needn't show every extreme that they name: `span_start`: each multiple of 128 below 4096 appears once. Entries 2 k and 2 k + 1 are the spans held by index k of ctx; they add up to 3968, the smaller first. lse[s, h, i] is the log of the sum of exp(scores[s, h, i, j]) over the j with positions[j] <= positions[i]. outputs[s, i, h] is the sum over j of probs[s, h, i, j] values[s, j], rounded once.
All inputs are finite; a program needn't handle non-finite values.
Results may differ from a plain program's by a relative error of at most 0.014.
Values may be sent and summed in bfloat16 or wider, within the bound.
A program may use at most 64 MiB of HBM per device.

v0:
```python
import jax
import jax.numpy as jnp
from jax import lax
from jax.sharding import PartitionSpec as P


def from_behind(shard, axis, by):
    length = lax.axis_size(axis)
    return lax.ppermute(shard, axis, [(i, (i + by) % length) for i in range(length)])


def tile_grads(
    query_rows, grad_rows, lse_rows, delta_rows, query_pos, key_rows, value_rows, key_pos
):
    score_scale = query_rows.shape[-1] ** (-0.5)
    scores = (
        jnp.einsum("rhd,cd->hrc", query_rows, key_rows, preferred_element_type=jnp.float32)
        * score_scale
    )
    allowed = key_pos[None, :] <= query_pos[:, None]
    probs = jnp.where(allowed[None], jnp.exp(scores - lse_rows[:, :, None]), 0.0)
    probs_low = probs.astype(jnp.bfloat16)
    grad_probs = jnp.einsum(
        "rhd,cd->hrc", grad_rows, value_rows, preferred_element_type=jnp.float32
    )
    grad_scores = (probs * (grad_probs - delta_rows[:, :, None])).astype(jnp.bfloat16)
    query_grad = (
        jnp.einsum("hrc,cd->rhd", grad_scores, key_rows, preferred_element_type=jnp.float32)
        * score_scale
    )
    key_grad = (
        jnp.einsum("hrc,rhd->cd", grad_scores, query_rows, preferred_element_type=jnp.float32)
        * score_scale
    )
    value_grad = jnp.einsum("hrc,rhd->cd", probs_low, grad_rows, preferred_element_type=jnp.float32)
    return (query_grad, key_grad, value_grad)


def full_tile(operands):
    return tile_grads(
        operands[0],
        operands[1],
        operands[2],
        operands[3],
        operands[4],
        operands[5],
        operands[6],
        operands[7],
    )


def empty_grads(operands):
    query_rows = operands[0]
    key_rows = operands[5]
    return (
        jnp.zeros(query_rows.shape, jnp.float32),
        jnp.zeros(key_rows.shape, jnp.float32),
        jnp.zeros(key_rows.shape, jnp.float32),
    )


def sweep_keys(query_side, key_rows, value_rows):
    queries, grad_out, lse_rows, delta_rows, query_pos, own_starts, span_start = query_side
    row_count = queries.shape[0]
    span_rows = row_count // 2
    head_size = key_rows.shape[1]
    block_count = key_rows.shape[0] // row_count
    offsets = jnp.arange(span_rows, dtype=jnp.int32)
    query_init = jnp.zeros(queries.shape, jnp.float32)
    keys_init = jnp.zeros((key_rows.shape[0], 2 * head_size), jnp.float32)

    def sweep_turn(block_index, totals):
        query_total, key_total = totals
        key_block = lax.dynamic_slice_in_dim(key_rows, block_index * row_count, row_count, 0)
        value_block = lax.dynamic_slice_in_dim(value_rows, block_index * row_count, row_count, 0)
        block_starts = lax.dynamic_slice_in_dim(
            span_start, block_index * row_count // span_rows, 2, 0
        )
        query_parts = []
        key_parts = [
            jnp.zeros((span_rows, head_size), jnp.float32),
            jnp.zeros((span_rows, head_size), jnp.float32),
        ]
        value_parts = [
            jnp.zeros((span_rows, head_size), jnp.float32),
            jnp.zeros((span_rows, head_size), jnp.float32),
        ]
        for query_half in range(2):
            row_low = query_half * span_rows
            row_high = row_low + span_rows
            query_sum = jnp.zeros((span_rows,) + queries.shape[1:], jnp.float32)
            for key_half in range(2):
                key_low = key_half * span_rows
                key_high = key_low + span_rows
                operands = (
                    queries[row_low:row_high],
                    grad_out[row_low:row_high],
                    lse_rows[:, row_low:row_high],
                    delta_rows[:, row_low:row_high],
                    query_pos[row_low:row_high],
                    key_block[key_low:key_high],
                    value_block[key_low:key_high],
                    block_starts[key_half] + offsets,
                )
                tile_out = lax.cond(
                    block_starts[key_half] <= own_starts[query_half],
                    full_tile,
                    empty_grads,
                    operands,
                )
                query_sum = query_sum + tile_out[0]
                key_parts[key_half] = key_parts[key_half] + tile_out[1]
                value_parts[key_half] = value_parts[key_half] + tile_out[2]
            query_parts.append(query_sum)
        query_grad = jnp.concatenate(query_parts, axis=0)
        key_grad = jnp.concatenate(key_parts, axis=0)
        value_grad = jnp.concatenate(value_parts, axis=0)
        query_total = query_total + query_grad
        key_total = lax.dynamic_update_slice_in_dim(
            key_total, jnp.concatenate([key_grad, value_grad], axis=1), block_index * row_count, 0
        )
        return (query_total, key_total)

    return lax.fori_loop(0, block_count, sweep_turn, (query_init, keys_init))


def body(queries, keys, values, outputs, grad_held, lse, span_start):
    grad_next = from_behind(grad_held, "section", -1)
    query_block = queries[0]
    key_block = keys[0]
    value_block = values[0]
    row_count = query_block.shape[0]
    span_rows = row_count // 2
    head_size = key_block.shape[1]
    context = lax.axis_index("ctx")
    own_starts = lax.dynamic_slice_in_dim(span_start, 2 * context, 2, 0)
    offsets = jnp.arange(span_rows, dtype=jnp.int32)
    query_pos = (own_starts[:, None] + offsets[None, :]).reshape(row_count)
    grad_out = grad_next[0]
    delta_rows = jnp.sum(grad_out.astype(jnp.float32) * outputs[0].astype(jnp.float32), axis=-1).T
    query_side = (query_block, grad_out, lse[0], delta_rows, query_pos, own_starts, span_start)
    query_add, key_value_part = sweep_keys(
        query_side,
        lax.all_gather(key_block, "ctx", axis=0, tiled=True),
        lax.all_gather(value_block, "ctx", axis=0, tiled=True),
    )
    key_value_full = key_value_part
    query_total, key_value_full = (query_add, key_value_full)
    summed = lax.psum_scatter(
        key_value_full.astype(jnp.bfloat16), "ctx", scatter_dimension=0, tiled=True
    ).astype(jnp.float32)
    query_out = query_total.astype(jnp.bfloat16)[None]
    key_out = summed[:, :head_size].astype(jnp.bfloat16)[None]
    value_out = summed[:, head_size:].astype(jnp.bfloat16)[None]
    return (query_out, key_out, value_out)


def solution(mesh):
    placed = (
        P("section", "ctx", None, None),
        P("section", "ctx", None),
        P("section", "ctx", None),
        P("section", "ctx", None, None),
        P("section", "ctx", None, None),
        P("section", None, "ctx"),
        P(),
    )
    return jax.shard_map(
        body,
        mesh=mesh,
        in_specs=placed,
        out_specs=(
            P("section", "ctx", None, None),
            P("section", "ctx", None),
            P("section", "ctx", None),
        ),
        check_vma=False,
    )
```

profile of v0, /device:TPU:2, one launch (start us, length us, event | category | flops | bytes accessed | tf_op | source)
XLA Modules:
  0.0 635.1 jit_solution(2357705479401431310)
XLA Ops:
  8.7 2.6 copy.15
  17.2 19.2 %collective-permute-done = bf16[1,256,16,128]{3,1,2,0:T(8,128)(2,1)S(1)} collective-permute-done((bf16[1,256,16,128]{3,1,2,0:T(8,128)(2,1)}, bf16[1,256,16,128]{3,1,2,0:T(8,128)(2,1)S(1)}, u32[]{:S(2)}, u32[]{:S(2)}) %collective-permute-start) | collective-permute-done | bytes 1048608 | tf_op jit(solution)/shard_map/ppermute | solution.py:9
  37.1 44.0 %all-gather.5.cloned.1.call-done = bf16[1,4096,128]{2,1,0:T(8,128)(2,1)} async-done(((bf16[1,256,128]{2,1,0:T(8,128)(2,1)}), bf16[1,4096,128]{2,1,0:T(8,128)(2,1)}) %all-gather.5.cloned.1.call-update) | async-done | bytes 1048592 | tf_op jit(solution)/shard_map/all_gather | solution.py:144
  81.1 53.9 %all-gather.7.cloned.1.call-done = bf16[1,4096,128]{2,1,0:T(8,128)(2,1)} async-done(((bf16[1,256,128]{2,1,0:T(8,128)(2,1)}), bf16[1,4096,128]{2,1,0:T(8,128)(2,1)}) %all-gather.7.cloned.1.call-update) | async-done | bytes 1048592 | tf_op jit(solution)/shard_map/all_gather | solution.py:145
  136.5 407.7 %while.19 = (s32[]{:T(128)}, f32[256,16,128]{2,0,1:T(8,128)}, bf16[4096,256]{1,0:T(8,128)(2,1)}, s32[32]{0:T(128)}, s32[2]{0:T(128)}, /*index=5*/bf16[4096,128]{...) while((s32[]{:T(128)}, f32[256,16,128]{2,0,1:T(8,128)}, ...), condition=%wide.region_10.11_spmd.clone.clone, body=%wide.region_1.10_spmd.clone.clone.sunk | while | flops 1353384192 | bytes 84388064 | solution.py:124
  154.0 2.4 conditional.16
  181.9 2.4 conditional.17
  204.9 2.4 conditional.16
  207.3 2.4 conditional.17
  232.7 2.4 conditional.17
  255.7 2.4 conditional.16
  258.2 2.4 conditional.17
  283.6 2.4 conditional.17
  306.6 2.4 conditional.16
  334.4 2.4 conditional.17
  357.5 2.4 conditional.16
  385.3 2.4 conditional.17
  408.3 2.4 conditional.16
  435.3 2.4 conditional.16
  460.9 2.4 conditional.17
  486.4 2.4 conditional.17
  509.4 2.4 conditional.16
  537.2 2.4 conditional.17
  548.0 79.1 %reduce-scatter.2.cloned.1.call-done = bf16[256,256]{1,0:T(8,128)(2,1)} async-done(((bf16[4096,256]{1,0:T(8,128)(2,1)}), bf16[256,256]{1,0:T(8,128)(2,1)}) %reduce-scatter.2.cloned.1.call-update) | async-done | bytes 131088 | tf_op jit(solution)/shard_map/reduce_scatter | solution.py:149
  (936 shorter events, 369.9 us)
Async XLA Ops:
  7.2 73.9 %all-gather.5.cloned.1.call-start = ((), (), s32[]{:S(2)}) async-start(), calls=%async_computation.2 | async-start | bytes 1114112 | tf_op jit(solution)/shard_map/all_gather | solution.py:144
  7.9 127.1 %all-gather.7.cloned.1.call-start = ((), (), s32[]{:S(2)}) async-start(), calls=%async_computation.3 | async-start | bytes 1114112 | tf_op jit(solution)/shard_map/all_gather | solution.py:145
  8.7 27.7 %copy-start.9 = (bf16[1,256,16,128]{3,2,1,0:T(8,128)(2,1)S(1)}, bf16[1,256,16,128]{3,2,1,0:T(8,128)(2,1)}, u32[]{:S(2)}) copy-start(bf16[1,256,16,128]{3,2,1,0:T(8,128)(2,1)} %param.20) | copy-start | bytes 3145732
  8.7 618.4 %reduce-scatter.2.cloned.1.call-start = ((), (), s32[]{:S(2)}) async-start(), calls=%async_computation.1 | async-start | bytes 2228224 | tf_op jit(solution)/shard_map/reduce_scatter | solution.py:149
  11.3 25.1 %collective-permute-start = (bf16[1,256,16,128]{3,1,2,0:T(8,128)(2,1)}, bf16[1,256,16,128]{3,1,2,0:T(8,128)(2,1)S(1)}, u32[]{:S(2)}, u32[]{:S(2)}) collective-permute-start(bf16[1,256,16,128]{3,1,2,0:T(8,128)(2,1)} %copy.15), channel_id=1, source_target_pairs={{0,240},{16,0},{32,16},{48,32},{64,48},{80,64},{96,80},{112,96},{1... | collective-permute-start | bytes 3145736 | tf_op jit(solution)/shard_map/ppermute | solution.py:9
  17.2 119.3 %copy-start.12 = (f32[1,16,256]{2,1,0:T(8,128)S(1)}, f32[1,16,256]{2,1,0:T(8,128)}, u32[]{:S(2)}) copy-start(f32[1,16,256]{2,1,0:T(8,128)} %param.22) | copy-start | bytes 49156
  163.4 13.3 %copy-start.5 = (bf16[256,16,128]{2,0,1:T(8,128)(2,1)}, bf16[256,16,128]{2,0,1:T(8,128)(2,1)S(1)}, u32[]{:S(2)}) copy-start(bf16[256,16,128]{2,0,1:T(8,128)(2,1)S(1)} %get-tuple-element.783) | copy-start | bytes 3145732 | tf_op jit(solution)/shard_map/while
  163.4 13.3 %copy-start.10 = (f32[16,256]{1,0:T(8,128)}, f32[16,256]{1,0:T(8,128)S(1)}, u32[]{:S(2)}) copy-start(f32[16,256]{1,0:T(8,128)S(1)} %get-tuple-element.784) | copy-start | bytes 49156 | tf_op jit(solution)/shard_map/while
  188.8 13.3 %copy-start.5 = (bf16[256,16,128]{2,0,1:T(8,128)(2,1)}, bf16[256,16,128]{2,0,1:T(8,128)(2,1)S(1)}, u32[]{:S(2)}) copy-start(bf16[256,16,128]{2,0,1:T(8,128)(2,1)S(1)} %get-tuple-element.783) | copy-start | bytes 3145732 | tf_op jit(solution)/shard_map/while
  188.8 13.3 %copy-start.10 = (f32[16,256]{1,0:T(8,128)}, f32[16,256]{1,0:T(8,128)S(1)}, u32[]{:S(2)}) copy-start(f32[16,256]{1,0:T(8,128)S(1)} %get-tuple-element.784) | copy-start | bytes 49156 | tf_op jit(solution)/shard_map/while
  214.2 13.3 %copy-start.5 = (bf16[256,16,128]{2,0,1:T(8,128)(2,1)}, bf16[256,16,128]{2,0,1:T(8,128)(2,1)S(1)}, u32[]{:S(2)}) copy-start(bf16[256,16,128]{2,0,1:T(8,128)(2,1)S(1)} %get-tuple-element.783) | copy-start | bytes 3145732 | tf_op jit(solution)/shard_map/while
  214.2 13.3 %copy-start.10 = (f32[16,256]{1,0:T(8,128)}, f32[16,256]{1,0:T(8,128)S(1)}, u32[]{:S(2)}) copy-start(f32[16,256]{1,0:T(8,128)S(1)} %get-tuple-element.784) | copy-start | bytes 49156 | tf_op jit(solution)/shard_map/while
  239.7 13.3 %copy-start.10 = (f32[16,256]{1,0:T(8,128)}, f32[16,256]{1,0:T(8,128)S(1)}, u32[]{:S(2)}) copy-start(f32[16,256]{1,0:T(8,128)S(1)} %get-tuple-element.784) | copy-start | bytes 49156 | tf_op jit(solution)/shard_map/while
  265.1 13.3 %copy-start.10 = (f32[16,256]{1,0:T(8,128)}, f32[16,256]{1,0:T(8,128)S(1)}, u32[]{:S(2)}) copy-start(f32[16,256]{1,0:T(8,128)S(1)} %get-tuple-element.784) | copy-start | bytes 49156 | tf_op jit(solution)/shard_map/while
  290.5 13.3 %copy-start.10 = (f32[16,256]{1,0:T(8,128)}, f32[16,256]{1,0:T(8,128)S(1)}, u32[]{:S(2)}) copy-start(f32[16,256]{1,0:T(8,128)S(1)} %get-tuple-element.784) | copy-start | bytes 49156 | tf_op jit(solution)/shard_map/while
  316.0 13.3 %copy-start.10 = (f32[16,256]{1,0:T(8,128)}, f32[16,256]{1,0:T(8,128)S(1)}, u32[]{:S(2)}) copy-start(f32[16,256]{1,0:T(8,128)S(1)} %get-tuple-element.784) | copy-start | bytes 49156 | tf_op jit(solution)/shard_map/while
  341.4 13.3 %copy-start.10 = (f32[16,256]{1,0:T(8,128)}, f32[16,256]{1,0:T(8,128)S(1)}, u32[]{:S(2)}) copy-start(f32[16,256]{1,0:T(8,128)S(1)} %get-tuple-element.784) | copy-start | bytes 49156 | tf_op jit(solution)/shard_map/while
  366.8 13.3 %copy-start.10 = (f32[16,256]{1,0:T(8,128)}, f32[16,256]{1,0:T(8,128)S(1)}, u32[]{:S(2)}) copy-start(f32[16,256]{1,0:T(8,128)S(1)} %get-tuple-element.784) | copy-start | bytes 49156 | tf_op jit(solution)/shard_map/while
  392.3 13.3 %copy-start.10 = (f32[16,256]{1,0:T(8,128)}, f32[16,256]{1,0:T(8,128)S(1)}, u32[]{:S(2)}) copy-start(f32[16,256]{1,0:T(8,128)S(1)} %get-tuple-element.784) | copy-start | bytes 49156 | tf_op jit(solution)/shard_map/while
  417.7 13.3 %copy-start.10 = (f32[16,256]{1,0:T(8,128)}, f32[16,256]{1,0:T(8,128)S(1)}, u32[]{:S(2)}) copy-start(f32[16,256]{1,0:T(8,128)S(1)} %get-tuple-element.784) | copy-start | bytes 49156 | tf_op jit(solution)/shard_map/while
  442.5 13.3 %copy-start.10 = (f32[16,256]{1,0:T(8,128)}, f32[16,256]{1,0:T(8,128)S(1)}, u32[]{:S(2)}) copy-start(f32[16,256]{1,0:T(8,128)S(1)} %get-tuple-element.784) | copy-start | bytes 49156 | tf_op jit(solution)/shard_map/while
  467.9 13.3 %copy-start.10 = (f32[16,256]{1,0:T(8,128)}, f32[16,256]{1,0:T(8,128)S(1)}, u32[]{:S(2)}) copy-start(f32[16,256]{1,0:T(8,128)S(1)} %get-tuple-element.784) | copy-start | bytes 49156 | tf_op jit(solution)/shard_map/while
  493.3 13.3 %copy-start.10 = (f32[16,256]{1,0:T(8,128)}, f32[16,256]{1,0:T(8,128)S(1)}, u32[]{:S(2)}) copy-start(f32[16,256]{1,0:T(8,128)S(1)} %get-tuple-element.784) | copy-start | bytes 49156 | tf_op jit(solution)/shard_map/while
  518.8 13.3 %copy-start.10 = (f32[16,256]{1,0:T(8,128)}, f32[16,256]{1,0:T(8,128)S(1)}, u32[]{:S(2)}) copy-start(f32[16,256]{1,0:T(8,128)S(1)} %get-tuple-element.784) | copy-start | bytes 49156 | tf_op jit(solution)/shard_map/while
  (144 other events, 426.0 us)
Sparse Core Ops, SparseCore 0:
  10.7 70.3 all-gather.4
  83.8 51.1 all-gather.6
  544.4 82.6 reduce-scatter.1
where the time goes:
time: 640 us; the launch traced here: 635 us
  waiting for transfers between devices  198 us (31%)
  other arithmetic  142 us (22%)
  local copies, waits for them, and re-layouts  137 us (21%)
  loops' own time  91.4 us (14%)
  matrix products  51.3 us (8%)
  between operations  13.8 us (2%)
    another operation x1, loops' own time, sweep_keys(): return lax.fori_loop(0, block_count, sweep_turn, (query_init, keys_init))  88.3 us
    reduce_scatter x1, waiting for transfers between devices, body(): lax.psum_scatter(key_value_full.astype(jnp.bfloat16), 'ctx', scatter_dime...  79.1 us
    all_gather x1, waiting for transfers between devices, body(): lax.all_gather(value_block, 'ctx', axis=0, tiled=True)  53.9 us
    while x320, local copies, waits for them, and re-layouts  44.6 us
    all_gather x1, waiting for transfers between devices, body(): lax.all_gather(key_block, 'ctx', axis=0, tiled=True)  44 us
    add x32, other arithmetic, sweep_turn(): query_sum = query_sum + tile_out[0]  42.8 us
    slice x16, other arithmetic, sweep_turn(): query_pos[row_low:row_high]  31.5 us
    le x33, other arithmetic, tile_grads(): allowed = key_pos[None, :] <= query_pos[:, None]  23.8 us
  transfers between devices with their start and end apart: 4, of which 4 were waited for; matrix products, arithmetic and copies ran while one was open for 1% of the time, Pallas kernels for 0%

commit v1 on v0

--- a/solution.py
+++ b/solution.py
@@ -141,7 +141,9 @@
     query_side = (query_block, grad_out, lse[0], delta_rows, query_pos, own_starts, span_start)
     query_add, key_value_part = sweep_keys(
         query_side,
-        lax.all_gather(key_block, "ctx", axis=0, tiled=True),
+        jnp.concatenate(
+            lax.all_to_all(jnp.stack(lax.axis_size("ctx") * [key_block]), "ctx", 0, 0), axis=0
+        ),
         lax.all_gather(value_block, "ctx", axis=0, tiled=True),
     )
     key_value_full = key_value_part

time: 640 us -> 578 us (0.903)
  waiting for transfers between devices: 198 us -> 137 us
  starting transfers between devices: 2.36 us -> 12 us
  loops' own time: 91.4 us -> 83.9 us
    all_gather x1 -> x0, waiting for transfers between devices: 44 us -> none  [body(): lax.all_gather(key_block, 'ctx', axis=0, tiled=True)]
    all_gather x1, waiting for transfers between devices: 53.9 us -> 24.5 us  [body(): lax.all_gather(value_block, 'ctx', axis=0, tiled=True)]
    all_to_all x0 -> x1, starting transfers between devices: none -> 11.4 us  [body(): lax.all_to_all(jnp.stack(lax.axis_size('ctx') * [key_block]), 'ctx', 0, 0)]
    reduce_scatter x1, waiting for transfers between devices: 79.1 us -> 90.3 us  [body(): lax.psum_scatter(key_value_full.astype(jnp.bfloat16), 'ctx', scatter_dime...]
    another operation x1, loops' own time: 88.3 us -> 80.8 us  [sweep_keys(): return lax.fori_loop(0, block_count, sweep_turn, (query_init, keys_init))]
  transfers between devices with their start and end apart: 4 -> 4, of which waited for: 4 -> 3; matrix products, arithmetic and copies ran while one was open for 1% -> 2% of each run, Pallas kernels for 0% -> 0%
where the time goes in v1:
time: 578 us; the launch traced here: 573 us
  other arithmetic  141 us (24%)
  waiting for transfers between devices  137 us (24%)
  local copies, waits for them, and re-layouts  134 us (23%)
  loops' own time  83.9 us (15%)
  matrix products  51.4 us (9%)
  between operations  14.1 us (2%)
  starting transfers between devices  12 us (2%)
    reduce_scatter x1, waiting for transfers between devices, body(): lax.psum_scatter(key_value_full.astype(jnp.bfloat16), 'ctx', scatter_dime...  90.3 us
    another operation x1, loops' own time, sweep_keys(): return lax.fori_loop(0, block_count, sweep_turn, (query_init, keys_init))  80.8 us
    add x32, other arithmetic, sweep_turn(): query_sum = query_sum + tile_out[0]  43.5 us
    while x320, local copies, waits for them, and re-layouts  41.3 us
    slice x16, other arithmetic, sweep_turn(): query_pos[row_low:row_high]  30.2 us
    all_gather x1, waiting for transfers between devices, body(): lax.all_gather(value_block, 'ctx', axis=0, tiled=True)  24.5 us
    le x33, other arithmetic, tile_grads(): allowed = key_pos[None, :] <= query_pos[:, None]  22.5 us
    slice x16, local copies, waits for them, and re-layouts, sweep_turn(): grad_out[row_low:row_high]  21.5 us
  transfers between devices with their start and end apart: 4, of which 3 were waited for; matrix products, arithmetic and copies ran while one was open for 2% of the time, Pallas kernels for 0%

profile of v1, /device:TPU:2, one launch (start us, length us, event | category | flops | bytes accessed | tf_op | source)
XLA Modules:
  0.0 572.9 jit_solution(7990362391594796757)
XLA Ops:
  9.9 11.4 %all-to-all-start = ((bf16[16,256,128]{2,1,0:T(8,128)(2,1)}), bf16[16,256,128]{2,1,0:T(8,128)(2,1)}, u32[]{:S(2)}, u32[]{:S(2)}) async-start(bf16[16,256,128]{2,1,0:T(8,128)(2,1)} %stack.3), calls=%async_computation | async-start | bytes 2097152 | tf_op jit(solution)/shard_map/all_to_all | solution.py:145
  26.9 21.3 %collective-permute-done = bf16[1,256,16,128]{3,1,2,0:T(8,128)(2,1)S(1)} collective-permute-done((bf16[1,256,16,128]{3,1,2,0:T(8,128)(2,1)}, bf16[1,256,16,128]{3,1,2,0:T(8,128)(2,1)S(1)}, u32[]{:S(2)}, u32[]{:S(2)}) %collective-permute-start) | collective-permute-done | bytes 1048608 | tf_op jit(solution)/shard_map/ppermute | solution.py:9
  50.1 24.5 %all-gather.3.cloned.1.call-done = bf16[1,4096,128]{2,1,0:T(8,128)(2,1)} async-done(((bf16[1,256,128]{2,1,0:T(8,128)(2,1)}), bf16[1,4096,128]{2,1,0:T(8,128)(2,1)}) %all-gather.3.cloned.1.call-update) | async-done | bytes 1048592 | tf_op jit(solution)/shard_map/all_gather | solution.py:147
  76.1 394.3 %while.19 = (s32[]{:T(128)}, f32[256,16,128]{2,0,1:T(8,128)}, bf16[4096,256]{1,0:T(8,128)(2,1)}, s32[32]{0:T(128)}, s32[2]{0:T(128)}, /*index=5*/bf16[4096,128]{...) while((s32[]{:T(128)}, f32[256,16,128]{2,0,1:T(8,128)}, ...), condition=%wide.region_10.11_spmd.clone.clone, body=%wide.region_1.10_spmd.clone.clone.sunk | while | flops 1353384192 | bytes 84388064 | solution.py:124
  93.0 2.4 conditional.16
  95.4 2.3 conditional.17
  117.6 2.4 conditional.16
  142.1 2.4 conditional.16
  166.7 2.4 conditional.16
  191.3 2.4 conditional.16
  215.9 2.4 conditional.16
  240.5 2.4 conditional.16
  265.1 2.4 conditional.16
  289.7 2.4 conditional.16
  314.3 2.4 conditional.16
  338.9 2.4 conditional.16
  341.3 2.3 conditional.17
  365.0 2.4 conditional.16
  387.5 2.4 conditional.16
  412.0 2.4 conditional.16
  436.6 2.4 conditional.16
  439.0 2.3 conditional.17
  461.2 2.4 conditional.16
  474.3 90.3 %reduce-scatter.2.cloned.1.call-done = bf16[256,256]{1,0:T(8,128)(2,1)} async-done(((bf16[4096,256]{1,0:T(8,128)(2,1)}), bf16[256,256]{1,0:T(8,128)(2,1)}) %reduce-scatter.2.cloned.1.call-update) | async-done | bytes 131088 | tf_op jit(solution)/shard_map/reduce_scatter | solution.py:151
  (936 shorter events, 362.8 us)
Async XLA Ops:
  7.2 14.2 %copy-start.8 = (bf16[1,256,16,128]{3,2,1,0:T(8,128)(2,1)S(1)}, bf16[1,256,16,128]{3,2,1,0:T(8,128)(2,1)}, u32[]{:S(2)}) copy-start(bf16[1,256,16,128]{3,2,1,0:T(8,128)(2,1)} %param.21) | copy-start | bytes 3145732
  7.2 67.5 %all-gather.3.cloned.1.call-start = ((), (), s32[]{:S(2)}) async-start(), calls=%async_computation.3 | async-start | bytes 1114112 | tf_op jit(solution)/shard_map/all_gather | solution.py:147
  9.9 13.3 %copy-start.9 = (bf16[1,256,16,128]{3,2,1,0:T(8,128)(2,1)S(1)}, bf16[1,256,16,128]{3,2,1,0:T(8,128)(2,1)}, u32[]{:S(2)}) copy-start(bf16[1,256,16,128]{3,2,1,0:T(8,128)(2,1)} %param.17) | copy-start | bytes 3145732
  9.9 64.7 %all-to-all-start = ((bf16[16,256,128]{2,1,0:T(8,128)(2,1)}), bf16[16,256,128]{2,1,0:T(8,128)(2,1)}, u32[]{:S(2)}, u32[]{:S(2)}) async-start(bf16[16,256,128]{2,1,0:T(8,128)(2,1)} %stack.3), calls=%async_computation | async-start | bytes 2097152 | tf_op jit(solution)/shard_map/all_to_all | solution.py:145
  21.3 543.2 %reduce-scatter.2.cloned.1.call-start = ((), (), s32[]{:S(2)}) async-start(), calls=%async_computation.2 | async-start | bytes 2228224 | tf_op jit(solution)/shard_map/reduce_scatter | solution.py:151
  22.6 25.6 %collective-permute-start = (bf16[1,256,16,128]{3,1,2,0:T(8,128)(2,1)}, bf16[1,256,16,128]{3,1,2,0:T(8,128)(2,1)S(1)}, u32[]{:S(2)}, u32[]{:S(2)}) collective-permute-start(bf16[1,256,16,128]{3,1,2,0:T(8,128)(2,1)} %copy.15), channel_id=1, source_target_pairs={{0,240},{16,0},{32,16},{48,32},{64,48},{80,64},{96,80},{112,96},{1... | collective-permute-start | bytes 3145736 | tf_op jit(solution)/shard_map/ppermute | solution.py:9
  26.9 49.2 %copy-start.12 = (f32[1,16,256]{2,1,0:T(8,128)S(1)}, f32[1,16,256]{2,1,0:T(8,128)}, u32[]{:S(2)}) copy-start(f32[1,16,256]{2,1,0:T(8,128)} %param.22) | copy-start | bytes 49156
  102.2 12.7 %copy-start.5 = (bf16[256,16,128]{2,0,1:T(8,128)(2,1)}, bf16[256,16,128]{2,0,1:T(8,128)(2,1)S(1)}, u32[]{:S(2)}) copy-start(bf16[256,16,128]{2,0,1:T(8,128)(2,1)S(1)} %get-tuple-element.783) | copy-start | bytes 3145732 | tf_op jit(solution)/shard_map/while
  102.2 12.7 %copy-start.10 = (f32[16,256]{1,0:T(8,128)}, f32[16,256]{1,0:T(8,128)S(1)}, u32[]{:S(2)}) copy-start(f32[16,256]{1,0:T(8,128)S(1)} %get-tuple-element.784) | copy-start | bytes 49156 | tf_op jit(solution)/shard_map/while
  126.8 12.7 %copy-start.5 = (bf16[256,16,128]{2,0,1:T(8,128)(2,1)}, bf16[256,16,128]{2,0,1:T(8,128)(2,1)S(1)}, u32[]{:S(2)}) copy-start(bf16[256,16,128]{2,0,1:T(8,128)(2,1)S(1)} %get-tuple-element.783) | copy-start | bytes 3145732 | tf_op jit(solution)/shard_map/while
  126.8 12.7 %copy-start.10 = (f32[16,256]{1,0:T(8,128)}, f32[16,256]{1,0:T(8,128)S(1)}, u32[]{:S(2)}) copy-start(f32[16,256]{1,0:T(8,128)S(1)} %get-tuple-element.784) | copy-start | bytes 49156 | tf_op jit(solution)/shard_map/while
  151.4 12.7 %copy-start.10 = (f32[16,256]{1,0:T(8,128)}, f32[16,256]{1,0:T(8,128)S(1)}, u32[]{:S(2)}) copy-start(f32[16,256]{1,0:T(8,128)S(1)} %get-tuple-element.784) | copy-start | bytes 49156 | tf_op jit(solution)/shard_map/while
  176.0 12.7 %copy-start.10 = (f32[16,256]{1,0:T(8,128)}, f32[16,256]{1,0:T(8,128)S(1)}, u32[]{:S(2)}) copy-start(f32[16,256]{1,0:T(8,128)S(1)} %get-tuple-element.784) | copy-start | bytes 49156 | tf_op jit(solution)/shard_map/while
  200.6 12.7 %copy-start.10 = (f32[16,256]{1,0:T(8,128)}, f32[16,256]{1,0:T(8,128)S(1)}, u32[]{:S(2)}) copy-start(f32[16,256]{1,0:T(8,128)S(1)} %get-tuple-element.784) | copy-start | bytes 49156 | tf_op jit(solution)/shard_map/while
  225.2 12.7 %copy-start.10 = (f32[16,256]{1,0:T(8,128)}, f32[16,256]{1,0:T(8,128)S(1)}, u32[]{:S(2)}) copy-start(f32[16,256]{1,0:T(8,128)S(1)} %get-tuple-element.784) | copy-start | bytes 49156 | tf_op jit(solution)/shard_map/while
  249.7 12.7 %copy-start.10 = (f32[16,256]{1,0:T(8,128)}, f32[16,256]{1,0:T(8,128)S(1)}, u32[]{:S(2)}) copy-start(f32[16,256]{1,0:T(8,128)S(1)} %get-tuple-element.784) | copy-start | bytes 49156 | tf_op jit(solution)/shard_map/while
  274.3 12.7 %copy-start.10 = (f32[16,256]{1,0:T(8,128)}, f32[16,256]{1,0:T(8,128)S(1)}, u32[]{:S(2)}) copy-start(f32[16,256]{1,0:T(8,128)S(1)} %get-tuple-element.784) | copy-start | bytes 49156 | tf_op jit(solution)/shard_map/while
  298.9 12.7 %copy-start.10 = (f32[16,256]{1,0:T(8,128)}, f32[16,256]{1,0:T(8,128)S(1)}, u32[]{:S(2)}) copy-start(f32[16,256]{1,0:T(8,128)S(1)} %get-tuple-element.784) | copy-start | bytes 49156 | tf_op jit(solution)/shard_map/while
  323.5 12.7 %copy-start.10 = (f32[16,256]{1,0:T(8,128)}, f32[16,256]{1,0:T(8,128)S(1)}, u32[]{:S(2)}) copy-start(f32[16,256]{1,0:T(8,128)S(1)} %get-tuple-element.784) | copy-start | bytes 49156 | tf_op jit(solution)/shard_map/while
  348.1 12.7 %copy-start.10 = (f32[16,256]{1,0:T(8,128)}, f32[16,256]{1,0:T(8,128)S(1)}, u32[]{:S(2)}) copy-start(f32[16,256]{1,0:T(8,128)S(1)} %get-tuple-element.784) | copy-start | bytes 49156 | tf_op jit(solution)/shard_map/while
  372.1 12.7 %copy-start.10 = (f32[16,256]{1,0:T(8,128)}, f32[16,256]{1,0:T(8,128)S(1)}, u32[]{:S(2)}) copy-start(f32[16,256]{1,0:T(8,128)S(1)} %get-tuple-element.784) | copy-start | bytes 49156 | tf_op jit(solution)/shard_map/while
  396.7 12.7 %copy-start.10 = (f32[16,256]{1,0:T(8,128)}, f32[16,256]{1,0:T(8,128)S(1)}, u32[]{:S(2)}) copy-start(f32[16,256]{1,0:T(8,128)S(1)} %get-tuple-element.784) | copy-start | bytes 49156 | tf_op jit(solution)/shard_map/while
  421.3 12.7 %copy-start.10 = (f32[16,256]{1,0:T(8,128)}, f32[16,256]{1,0:T(8,128)S(1)}, u32[]{:S(2)}) copy-start(f32[16,256]{1,0:T(8,128)S(1)} %get-tuple-element.784) | copy-start | bytes 49156 | tf_op jit(solution)/shard_map/while
  445.9 12.7 %copy-start.10 = (f32[16,256]{1,0:T(8,128)}, f32[16,256]{1,0:T(8,128)S(1)}, u32[]{:S(2)}) copy-start(f32[16,256]{1,0:T(8,128)S(1)} %get-tuple-element.784) | copy-start | bytes 49156 | tf_op jit(solution)/shard_map/while
  (144 other events, 420.1 us)
Sparse Core Ops, SparseCore 0:
  10.7 63.9 all-gather.2
  470.6 93.8 reduce-scatter.1
